TPU v7x, 32 devices: a whole 2x2x4 slice. The times are simulated.
32 devices in a mesh: dp: 8 (over y, x, core), mp: 4 (over z).
Axes of the slice: x: 2, y: 2, z: 4, core: 2. Of those that a mesh axis runs over, the one named last changes fastest.
Arguments:
- features: bfloat16 [4, 4096, 1152], P('mp', 'dp'), may hold values from -6 to 6
- context_gain: float32 [1152], replicated, may hold values from 0.1 to 1.9
- queries: bfloat16 [64, 1536], replicated, may hold values from -136 to 136
- w_key: bfloat16 [1152, 384], replicated, may hold values from -0.1875 to 0.1875
- w_value: bfloat16 [1152, 384], replicated, may hold values from -0.1875 to 0.1875
- w_out: bfloat16 [1536, 2048], replicated, may hold values from -0.15625 to 0.15625
- image_tiles: int32 [4, 2], P('mp'), may hold values from 1024 to 3072, as said below
- slot_start: int32 [4, 2], P('mp'), may hold values from 0 to 64
- text_rows: bfloat16 [4, 1024, 2048], P('mp', 'dp'), may hold values from -6 to 6
- row_grads: bfloat16 [4, 1024, 2048], P('mp', 'dp'), may hold values from -6 to 6
Outputs:
- merged_rows: bfloat16 [4, 1024, 2048], P('mp', 'dp')
- query_grad: float32 [64, 1536], replicated
Inputs may be any that keep to these rules, and one draw needn't show every extreme that they name: `image_tiles`: the 2 images of a group fill its 4096 rows in order; every image takes 2 * 512 to 3072 rows, and in every group one image takes exactly 1024 and one exactly 3072.
All inputs are finite; a program needn't handle non-finite values.
Results may differ from a plain program's by a relative error of at most 0.005.
The roundings to bfloat16 on the way count: a program that leaves them out, or rounds other values in their place, can miss the bound.
Values may be sent and summed in bfloat16 or wider, within the bound.
A program may use at most 128 MiB of HBM per device.

v0:
```python
import jax
import jax.numpy as jnp
from jax import lax
from jax.sharding import PartitionSpec as P

HEADS = 16
HEAD = 96
KVH = 4
LAT = 64
DM = 2048
TOK_DEV = 512
epsilon = 1e-06


def prefix_2(value, axis, join, neutral, backward):
    count, mine = (lax.axis_size(axis), lax.axis_index(axis))
    pieces = jax.tree.map(lambda part: lax.all_gather(part, axis), value)
    if backward:
        pieces = jax.tree.map(lambda part: part[::-1], pieces)
        mine = count - 1 - mine
    so_far = jax.tree.map(
        lambda part, zero: jnp.full_like(part, 0) + jnp.asarray(zero, part.dtype), value, neutral
    )

    def lap(position, so_far):
        longer = join(so_far, jax.tree.map(lambda part: part[position], pieces))
        return jax.tree.map(lambda new, old: jnp.where(position < mine, new, old), longer, so_far)

    return lax.fori_loop(0, count - 1, lap, so_far)


def normalize(features, context_gain):
    widened = features.astype(jnp.float32)
    mean_square = jnp.mean(widened * widened, axis=-1, keepdims=True)
    return (widened * lax.rsqrt(mean_square + epsilon) * context_gain).astype(jnp.bfloat16)


def merge_partials(earlier, later):
    early_id, early_peak, early_total, early_sum = earlier
    late_id, late_peak, late_total, late_sum = later
    joint_peak = jnp.maximum(early_peak, late_peak)
    early_scale = jnp.exp(early_peak - joint_peak)
    late_scale = jnp.exp(late_peak - joint_peak)
    joined = (
        late_id,
        joint_peak,
        early_total * early_scale + late_total * late_scale,
        early_sum * early_scale[..., None] + late_sum * late_scale[..., None],
    )
    same_image = early_id == late_id
    keep_early = late_id < 0
    return jax.tree.map(
        lambda early_value, joint_value, late_value: jnp.where(
            keep_early, early_value, jnp.where(same_image, joint_value, late_value)
        ),
        earlier,
        joined,
        later,
    )


def take_nearest(earlier, later):
    return jax.tree.map(
        lambda early_value, late_value: jnp.where(later[0] >= 0, late_value, early_value),
        earlier,
        later,
    )


def partial_sums(scores, value_heads, mask):
    masked = jnp.where(mask, scores, -jnp.inf)
    row_peak = jnp.max(masked, axis=-1)
    row_peak = jnp.where(jnp.any(mask), row_peak, 0.0)
    weights = jnp.where(mask, jnp.exp(scores - row_peak[..., None]), 0.0)
    weight_total = jnp.sum(weights, axis=-1)
    summed = jnp.einsum(
        "gclr,rge->gcle",
        weights.astype(jnp.bfloat16),
        value_heads,
        preferred_element_type=jnp.float32,
    )
    return (row_peak, weight_total, summed)


def to_heads(rows):
    return rows.reshape(LAT, KVH, HEADS // KVH, HEAD).transpose(1, 2, 0, 3)


def on_device(
    features,
    context_gain,
    queries,
    w_key,
    w_value,
    w_out,
    image_tiles,
    slot_start,
    text_rows,
    row_grads,
):
    group_heads = HEADS // KVH
    scale = HEAD ** (-0.5)
    normed = normalize(features[0], context_gain)
    key_heads = (
        jnp.dot(normed, w_key, preferred_element_type=jnp.float32)
        .astype(jnp.bfloat16)
        .reshape(TOK_DEV, KVH, HEAD)
    )
    value_heads = (
        jnp.dot(normed, w_value, preferred_element_type=jnp.float32)
        .astype(jnp.bfloat16)
        .reshape(TOK_DEV, KVH, HEAD)
    )
    query_heads = queries.reshape(LAT, KVH, group_heads, HEAD)
    scores = (
        jnp.einsum("lgce,rge->gclr", query_heads, key_heads, preferred_element_type=jnp.float32)
        * scale
    )
    device = lax.axis_index("dp")
    first_row = device * TOK_DEV
    image_ends = jnp.cumsum(image_tiles[0])
    positions = first_row + jnp.arange(TOK_DEV, dtype=jnp.int32)
    image_of = jnp.sum((positions[:, None] >= image_ends[None, :]).astype(jnp.int32), axis=1)
    first_image = image_of[0]
    last_image = image_of[-1]
    in_first = image_of == first_image
    in_last = (image_of == last_image) & (last_image != first_image)
    first_part = partial_sums(scores, value_heads, in_first)
    last_part = partial_sums(scores, value_heads, in_last)
    same_image = first_image == last_image
    running_part = jax.tree.map(
        lambda first_value, last_value: jnp.where(same_image, first_value, last_value),
        first_part,
        last_part,
    )
    element = (last_image.astype(jnp.float32),) + running_part
    stat_shape = (KVH, group_heads, LAT)
    identity = (
        jnp.full((), -1.0, jnp.float32),
        jnp.zeros(stat_shape, jnp.float32),
        jnp.zeros(stat_shape, jnp.float32),
        jnp.zeros(stat_shape + (HEAD,), jnp.float32),
    )
    prefix = prefix_2(element, "dp", merge_partials, identity, False)
    finished = merge_partials(prefix, (first_image.astype(jnp.float32),) + first_part)
    ends_here = image_ends[first_image] <= first_row + TOK_DEV
    attended = finished[3] / finished[2][..., None]
    attended_rows = attended.transpose(2, 0, 1, 3).reshape(LAT, HEADS * HEAD)
    projected = jnp.dot(
        attended_rows.astype(jnp.bfloat16), w_out, preferred_element_type=jnp.float32
    ).astype(jnp.bfloat16)
    slot_row = slot_start[0][first_image]
    placed = lax.dynamic_update_slice(text_rows[0], projected, (slot_row, jnp.int32(0)))
    merged = jnp.where(ends_here, placed, text_rows[0])[None]
    taken_rows = lax.dynamic_slice(row_grads[0], (slot_row, jnp.int32(0)), (LAT, DM))
    grad_rows = jnp.einsum(
        "ld,ed->le", taken_rows, w_out, preferred_element_type=jnp.float32
    ).astype(jnp.bfloat16)
    inner_dot = jnp.sum(to_heads(grad_rows.astype(jnp.float32)) * attended, axis=-1)
    valid_id = jnp.where(ends_here, first_image, -1).astype(jnp.float32)
    own_payload = (finished[1], finished[2], inner_dot, grad_rows)
    ident_whole = (
        jnp.full((), -1.0, jnp.float32),
        jnp.zeros(stat_shape, jnp.float32),
        jnp.zeros(stat_shape, jnp.float32),
        jnp.zeros(stat_shape, jnp.float32),
        jnp.zeros((LAT, HEADS * HEAD), jnp.float32),
    )
    suffix = prefix_2(
        (valid_id, finished[1], finished[2], inner_dot, grad_rows.astype(jnp.float32)),
        "dp",
        take_nearest,
        ident_whole,
        True,
    )
    far_payload = (suffix[1], suffix[2], suffix[3], suffix[4].astype(jnp.bfloat16))
    near_payload = jax.tree.map(
        lambda own_value, far_value: jnp.where(ends_here, own_value, far_value),
        own_payload,
        far_payload,
    )
    row_first = in_first[None, None, None, :]
    peak_rows = jnp.where(row_first, near_payload[0][..., None], far_payload[0][..., None])
    total_rows = jnp.where(row_first, near_payload[1][..., None], far_payload[1][..., None])
    inner_rows = jnp.where(row_first, near_payload[2][..., None], far_payload[2][..., None])
    probability = jnp.exp(scores - peak_rows) / total_rows
    dot_first = jnp.einsum(
        "gcle,rge->gclr", to_heads(near_payload[3]), value_heads, preferred_element_type=jnp.float32
    )
    dot_last = jnp.einsum(
        "gcle,rge->gclr", to_heads(far_payload[3]), value_heads, preferred_element_type=jnp.float32
    )
    chosen = jnp.where(row_first, dot_first, dot_last)
    score_grad = (probability * (chosen - inner_rows)).astype(jnp.bfloat16)
    grad_term = jnp.einsum(
        "gclr,rge->lgce", score_grad, key_heads, preferred_element_type=jnp.float32
    )
    grad_term = grad_term.reshape(LAT, HEADS * HEAD) * scale
    query_grad = lax.psum(grad_term, ("dp", "mp"))
    return (merged, query_grad)


def solution(mesh):
    placed = (
        P("mp", "dp", None),
        P(),
        P(),
        P(),
        P(),
        P(),
        P("mp", None),
        P("mp", None),
        P("mp", "dp", None),
        P("mp", "dp", None),
    )
    return jax.shard_map(
        on_device, mesh=mesh, in_specs=placed, out_specs=(P("mp", "dp", None), P()), check_vma=False
    )
```

profile of v0, /device:TPU:0, one launch (start us, length us, event | category | flops | bytes accessed | tf_op | source)
XLA Modules:
  0.0 310.1 jit_solution(13000130615180911)
XLA Ops:
  7.2 2.0 copy.83
  16.0 5.7 %convolution_convert_fusion = bf16[64,1536]{1,0:T(8,128)(2,1)} fusion(bf16[1536,2048]{1,0:T(8,128)(2,1)} %param.19, bf16[1,128,2048]{2,1,0:T(8,128)(2,1)} %param.23, s32[]{:T(128)S(6)} %select_n.443), kind=kOutput, calls=%fused_computation.23 | convolution fusion | flops 402751488 | bytes 6750212 | tf_op jit(solution)/shard_map/ld,ed->le/dot_general | solution.py:156
  25.7 2.1 fusion.67
  29.3 2.1 broadcast_select_fusion.7
  33.7 1.4 convolution_select_fusion
  40.0 15.9 %all-reduce.2 = (f32[8]{0:T(128)}, f32[8]{0:T(128)S(1)}) all-reduce(f32[8]{0:T(128)S(1)} %dynamic-update-slice.2, f32[8]{0:T(128)S(1)} %dynamic-update-slice.3), channel_id=1, replica_groups=mesh['dp'=8,'mp'=4] {'dp'}, use_global_device_ids=true, to_apply=%add | all-reduce | flops 16 | bytes 128
  56.6 1.2 reshape.122
  58.5 3.0 fusion.20
  61.5 8.3 %all-gather.1 = f32[32,4,64]{2,1,0:T(4,128)S(1)} all-gather(f32[4,4,64]{2,1,0:T(4,128)S(1)} %bitcast.201), channel_id=3, replica_groups=mesh['dp'=8,'mp'=4] {'dp'}, dimensions={0}, use_global_device_ids=true | all-gather | bytes 36864 | tf_op jit(solution)/shard_map/all_gather | solution.py:17
  69.8 9.4 %all-gather = f32[32,4,64]{2,1,0:T(4,128)S(1)} all-gather(f32[4,4,64]{2,1,0:T(4,128)S(1)} %copy-done.16), channel_id=2, replica_groups=mesh['dp'=8,'mp'=4] {'dp'}, dimensions={0}, use_global_device_ids=true | all-gather | bytes 36864 | tf_op jit(solution)/shard_map/all_gather | solution.py:17
  79.2 1.5 rev.19
  80.7 8.4 %all-gather.10.cloned.1.call-done = f32[32,4,64,96]{3,2,1,0:T(8,128)} async-done(((f32[4,4,64,96]{3,2,1,0:T(8,128)}), f32[32,4,64,96]{3,2,1,0:T(8,128)}) %all-gather.10.cloned.1.call-update) | async-done | bytes 3145744 | tf_op jit(solution)/shard_map/all_gather | solution.py:17
  89.1 33.9 %while.40 = (s32[]{:T(128)}, f32[]{:T(128)}, f32[4,4,64]{2,1,0:T(4,128)S(1)}, f32[4,4,64]{2,1,0:T(4,128)S(1)}, f32[4,4,64,96]{3,2,1,0:T(8,128)S(1)}, /*index=5*/...) while((s32[]{:T(128)}, f32[]{:T(128)}, ...), condition=%wide.region_10.11_spmd.clone, body=%wide.region_9.10_spmd.clone.sunk | while | flops 702472 | bytes 1220823 | solution.py:29
  91.7 1.6 select_select_fusion.14
  96.5 1.6 select_select_fusion.14
  101.4 1.6 select_select_fusion.14
  106.2 1.6 select_select_fusion.14
  111.1 1.6 select_select_fusion.14
  115.9 1.6 select_select_fusion.14
  120.8 1.6 select_select_fusion.14
  123.8 9.1 %all-gather.4 = f32[32,4,64]{2,1,0:T(4,128)S(1)} all-gather(f32[4,4,64]{2,1,0:T(4,128)S(1)} %bitcast.191), channel_id=6, replica_groups=mesh['dp'=8,'mp'=4] {'dp'}, dimensions={0}, use_global_device_ids=true | all-gather | bytes 36864 | tf_op jit(solution)/shard_map/all_gather | solution.py:17
  132.9 2.4 fusion.42
  135.3 8.4 %all-gather.5 = f32[32,4,64]{2,1,0:T(4,128)S(1)} all-gather(f32[4,4,64]{2,1,0:T(4,128)S(1)} %get-tuple-element.502), channel_id=7, replica_groups=mesh['dp'=8,'mp'=4] {'dp'}, dimensions={0}, use_global_device_ids=true | all-gather | bytes 36864 | tf_op jit(solution)/shard_map/all_gather | solution.py:17
  143.7 9.3 %all-gather.3 = f32[32,4,64]{2,1,0:T(4,128)S(1)} all-gather(f32[4,4,64]{2,1,0:T(4,128)S(1)} %bitcast.197), channel_id=5, replica_groups=mesh['dp'=8,'mp'=4] {'dp'}, dimensions={0}, use_global_device_ids=true | all-gather | bytes 36864 | tf_op jit(solution)/shard_map/all_gather | solution.py:17
  153.0 10.0 %while.41 = (s32[]{:T(128)}, f32[4,4,64]{2,1,0:T(4,128)S(1)}, f32[4,4,64]{2,1,0:T(4,128)S(1)}, f32[4,4,64]{2,1,0:T(4,128)S(1)}, bf16[64,1536]{1,0:T(8,128)(2,1)S...) while((s32[]{:T(128)}, f32[4,4,64]{2,1,0:T(4,128)S(1)}, ...), condition=%wide.region_13.14_spmd.clone, body=%wide.region_12.13_spmd.clone.sunk | while | flops 304133 | bytes 626881 | solution.py:29
  165.0 1.4 fusion.47
  166.4 3.9 %fusion.25 = f32[64,4,4,96]{3,0,2,1:T(8,128)} fusion(bf16[512,4,96,1]{0,2,3,1:T(8,128)(2,1)} %bitcast.208, f32[4,4,64,512]{3,2,1,0:T(8,128)S(1)} %fusion.47, f32[4,512,64,4]{1,2,3,0:T(8,128)} %copy-done.1, bf16[512,4,96,1]{0,2,3,1:T(8,128)(2,1)S(1)} %bitcast.180, f32[4,4,64]{2,1,0:T(4,128)S(1)} %get-tuple-element.368, f32[4,4,64]{2,1,0:T(4,128)S(1)} %bitcast.203, ...), kind=kOutput, calls=%fused_computation.52 | convolution fusion | flops 206143488 | bytes 5595648 | tf_op jit(solution)/shard_map/gclr,rge->lgce/dot_general | solution.py:195
  170.2 1.5 copy.28
  173.4 4.0 %fusion.8 = bf16[1,64,2048]{2,1,0:T(8,128)(2,1)S(1)} fusion(bf16[64,1536]{1,0:T(8,128)(2,1)S(1)} %convert_element_type.70, bf16[1536,2048]{1,0:T(8,128)(2,1)} %param.19, bf16[1,128,2048]{2,1,0:T(8,128)(2,1)S(1)} %copy-done.6, s32[]{:T(128)S(6)} %select_n.443, pred[]{:T(512)S(6)} %le.3), kind=kOutput, calls=%fused_computation.26 | convolution fusion | flops 402915328 | bytes 7012357 | tf_op jit(solution)/shard_map/dot_general | solution.py:149
  177.4 1.4 select_n.447
  178.8 123.0 %all-reduce.5.cloned.1.call-done = f32[64,1536]{1,0:T(8,128)} async-done(((f32[64,1536]{1,0:T(8,128)}), f32[64,1536]{1,0:T(8,128)}) %all-reduce.5.cloned.1.call-update) | async-done | bytes 393232 | tf_op jit(solution)/shard_map/psum | solution.py:199
  301.8 1.8 copy.85
  (136 shorter events, 29.8 us)
Async XLA Ops:
  7.2 20.6 %copy-start = (bf16[1152,384]{1,0:T(8,128)(2,1)S(1)}, bf16[1152,384]{1,0:T(8,128)(2,1)}, u32[]{:S(2)}) copy-start(bf16[1152,384]{1,0:T(8,128)(2,1)} %param.17) | copy-start | bytes 2654212
  7.2 72.0 %all-gather.12.cloned.1.call-start = ((), (), s32[]{:S(2)}) async-start(), calls=%async_computation.2 | async-start | bytes 1769472 | tf_op jit(solution)/shard_map/all_gather | solution.py:17
  16.0 8.4 %copy-start.12 = (bf16[64,1536]{1,0:T(8,128)(2,1)S(1)}, bf16[64,1536]{1,0:T(8,128)(2,1)}, u32[]{:S(2)}) copy-start(bf16[64,1536]{1,0:T(8,128)(2,1)} %param.16) | copy-start | bytes 589828
  16.0 9.4 %copy-start.8 = (bf16[1,512,1152]{2,1,0:T(8,128)(2,1)S(1)}, bf16[1,512,1152]{2,1,0:T(8,128)(2,1)}, u32[]{:S(2)}) copy-start(bf16[1,512,1152]{2,1,0:T(8,128)(2,1)} %param.14) | copy-start | bytes 3538948
  16.0 11.7 %copy-start.20 = (f32[1152]{0:T(1024)S(1)}, f32[1152]{0:T(1024)}, u32[]{:S(2)}) copy-start(f32[1152]{0:T(1024)} %param.15) | copy-start | bytes 13828
  21.7 67.4 %all-gather.10.cloned.1.call-start = ((), (), s32[]{:S(2)}) async-start(), calls=%async_computation.1 | async-start | bytes 4718592 | tf_op jit(solution)/shard_map/all_gather | solution.py:17
  25.7 3.0 copy-start.11
  27.7 30.7 %copy-start.17 = (pred[512]{0:T(512)(128)(4,1)}, pred[512]{0:T(512)(128)(4,1)S(1)}, u32[]{:S(2)}) copy-start(pred[512]{0:T(512)(128)(4,1)S(1)} %get-tuple-element.498) | copy-start | bytes 1540
  28.6 3.7 %copy-start.21 = (bf16[512,384]{0,1:T(8,128)(2,1)}, bf16[512,384]{0,1:T(8,128)(2,1)S(1)}, u32[]{:S(2)}) copy-start(bf16[512,384]{0,1:T(8,128)(2,1)S(1)} %convolution_convert_fusion.3) | copy-start | bytes 1179652
  28.6 2.8 copy-start.9
  28.6 2.8 copy-start.19
  29.3 3.6 %copy-start.1 = (f32[4,512,64,4]{1,2,3,0:T(8,128)}, f32[4,512,64,4]{1,2,3,0:T(8,128)S(1)}, u32[]{:S(2)}) copy-start(f32[4,512,64,4]{1,2,3,0:T(8,128)S(1)} %get-tuple-element.509) | copy-start | bytes 6291460
  31.4 27.1 %copy-start.13 = (f32[4,4,64]{2,1,0:T(4,128)}, f32[4,4,64]{2,1,0:T(4,128)S(1)}, u32[]{:S(2)}) copy-start(f32[4,4,64]{2,1,0:T(4,128)S(1)} %get-tuple-element.494) | copy-start | bytes 12292
  32.3 0.7 copy-start.4
  32.9 0.9 copy-start.3
  32.9 5.0 %copy-start.23 = (u32[32]{0:T(128)S(1)}, u32[32]{0:T(128)}, u32[]{:S(2)}) copy-start(u32[32]{0:T(128)} %constant.109) | copy-start | bytes 388
  32.9 23.7 %copy-start.2 = (bf16[64,1536]{1,0:T(8,128)(2,1)S(1)}, bf16[64,1536]{1,0:T(8,128)(2,1)}, u32[]{:S(2)}) copy-start(bf16[64,1536]{1,0:T(8,128)(2,1)} %convolution_convert_fusion) | copy-start | bytes 589828
  35.2 34.7 %copy-start.16 = (f32[4,4,64]{2,1,0:T(4,128)S(1)}, f32[4,4,64]{2,1,0:T(4,128)}, u32[]{:S(2)}) copy-start(f32[4,4,64]{2,1,0:T(4,128)} %get-tuple-element.492) | copy-start | bytes 12292
  35.2 266.6 %all-reduce.5.cloned.1.call-start = ((), (), s32[]{:S(2)}) async-start(), calls=%async_computation | async-start | bytes 786432 | tf_op jit(solution)/shard_map/psum | solution.py:199
  123.8 29.2 %copy-start.14 = (f32[2,8,64]{2,1,0:T(8,128)}, f32[2,8,64]{2,1,0:T(8,128)S(1)}, u32[]{:S(2)}) copy-start(f32[2,8,64]{2,1,0:T(8,128)S(1)} %get-tuple-element.536) | copy-start | bytes 12292
  123.8 29.2 %copy-start.22 = (f32[8]{0:T(128)S(1)}, f32[8]{0:T(128)}, u32[]{:S(2)}) copy-start(f32[8]{0:T(128)} %rev.15) | copy-start | bytes 100
  153.0 11.9 %copy-start.5 = (bf16[512,384]{0,1:T(8,128)(2,1)S(1)}, bf16[512,384]{0,1:T(8,128)(2,1)}, u32[]{:S(2)}) copy-start(bf16[512,384]{0,1:T(8,128)(2,1)} %copy-done.4) | copy-start | bytes 1179652
  163.0 3.3 %copy-start.15 = (f32[2,8,64]{2,1,0:T(8,128)S(1)}, f32[2,8,64]{2,1,0:T(8,128)}, u32[]{:S(2)}) copy-start(f32[2,8,64]{2,1,0:T(8,128)} %copy-done.14) | copy-start | bytes 12292
  163.0 3.3 %copy-start.18 = (pred[512]{0:T(512)(128)(4,1)S(1)}, pred[512]{0:T(512)(128)(4,1)}, u32[]{:S(2)}) copy-start(pred[512]{0:T(512)(128)(4,1)} %copy-done.17) | copy-start | bytes 1540
  170.2 2.7 copy-start.10
  170.2 3.2 %copy-start.6 = (bf16[1,128,2048]{2,1,0:T(8,128)(2,1)S(1)}, bf16[1,128,2048]{2,1,0:T(8,128)(2,1)}, u32[]{:S(2)}) copy-start(bf16[1,128,2048]{2,1,0:T(8,128)(2,1)} %copy.83) | copy-start | bytes 1572868
  178.8 124.8 %copy-start.7 = (bf16[1,128,2048]{2,1,0:T(8,128)(2,1)}, bf16[1,128,2048]{2,1,0:T(8,128)(2,1)S(1)}, u32[]{:S(2)}) copy-start(bf16[1,128,2048]{2,1,0:T(8,128)(2,1)S(1)} %select_n.447) | copy-start | bytes 1572868
Sparse Core Ops, SparseCore 0:
  21.9 28.3 all-gather.11
  52.2 36.9 all-gather.9
  173.0 128.6 all-reduce.4
where the time goes:
time: 311 us; the launch traced here: 310 us
  waiting for transfers between devices  131 us (42%)
  blocking collectives  60.4 us (19%)
  local copies, waits for them, and re-layouts  32.7 us (11%)
  other arithmetic  24.4 us (8%)
  between operations  23.5 us (8%)
  matrix products  19.2 us (6%)
  loops' own time  18.3 us (6%)
    psum x1, waiting for transfers between devices, on_device(): query_grad = lax.psum(grad_term, ('dp', 'mp'))  123 us
    all_gather x5, blocking collectives, prefix_2(): pieces = jax.tree.map(lambda part: lax.all_gather(part, axis), value)  44.5 us
    another operation x2, loops' own time, prefix_2(): return lax.fori_loop(0, count - 1, lap, so_far)  18.3 us
    unnamed x1, blocking collectives  15.9 us
    select_n x35, other arithmetic, lap(): jnp.where(position < mine, new, old)  12.8 us
    dynamic_slice x14, local copies, waits for them, and re-layouts, lap(): longer = join(so_far, jax.tree.map(lambda part: part[position], pieces))  12.8 us
    all_gather x2, waiting for transfers between devices, prefix_2(): pieces = jax.tree.map(lambda part: lax.all_gather(part, axis), value)  8.4 us
    unnamed x55, local copies, waits for them, and re-layouts  6.75 us
  transfers between devices with their start and end apart: 3, of which 2 were waited for; matrix products, arithmetic and copies ran while one was open for 8% of the time, Pallas kernels for 0%

commit v1 on v0

--- a/solution.py
+++ b/solution.py
@@ -196,7 +196,7 @@
         "gclr,rge->lgce", score_grad, key_heads, preferred_element_type=jnp.float32
     )
     grad_term = grad_term.reshape(LAT, HEADS * HEAD) * scale
-    query_grad = lax.psum(grad_term, ("dp", "mp"))
+    query_grad = jnp.sum(lax.all_gather(grad_term, ("dp", "mp")), axis=0)
     return (merged, query_grad)
 
 

time: 311 us -> 282 us (0.907)
  waiting for transfers between devices: 131 us -> 98 us
  other arithmetic: 24.4 us -> 30.5 us
    psum x1 -> x0, waiting for transfers between devices: 123 us -> none  [on_device(): query_grad = lax.psum(grad_term, ('dp', 'mp'))]
    all_gather x0 -> x1, waiting for transfers between devices: none -> 89.5 us  [on_device(): query_grad = jnp.sum(lax.all_gather(grad_term, ('dp', 'mp')), axis=0)]
    reduce_sum x0 -> x1, other arithmetic: none -> 6.18 us  [on_device(): query_grad = jnp.sum(lax.all_gather(grad_term, ('dp', 'mp')), axis=0)]
    unnamed x55 -> x54, local copies, waits for them, and re-layouts: 6.75 us -> 5.15 us
  transfers between devices with their start and end apart: 3 -> 3, of which waited for: 2 -> 2; matrix products, arithmetic and copies ran while one was open for 8% -> 9% of each run, Pallas kernels for 0% -> 0%
where the time goes in v1:
time: 282 us; the launch traced here: 281 us
  waiting for transfers between devices  98 us (35%)
  blocking collectives  60.5 us (21%)
  local copies, waits for them, and re-layouts  31.2 us (11%)
  other arithmetic  30.5 us (11%)
  between operations  23.2 us (8%)
  matrix products  19.2 us (7%)
  loops' own time  17.9 us (6%)
    all_gather x1, waiting for transfers between devices, on_device(): query_grad = jnp.sum(lax.all_gather(grad_term, ('dp', 'mp')), axis=0)  89.5 us
    all_gather x5, blocking collectives, prefix_2(): pieces = jax.tree.map(lambda part: lax.all_gather(part, axis), value)  44.5 us
    another operation x2, loops' own time, prefix_2(): return lax.fori_loop(0, count - 1, lap, so_far)  17.9 us
    unnamed x1, blocking collectives  16 us
    dynamic_slice x14, local copies, waits for them, and re-layouts, lap(): longer = join(so_far, jax.tree.map(lambda part: part[position], pieces))  12.9 us
    select_n x35, other arithmetic, lap(): jnp.where(position < mine, new, old)  12.8 us
    all_gather x2, waiting for transfers between devices, prefix_2(): pieces = jax.tree.map(lambda part: lax.all_gather(part, axis), value)  8.39 us
    reduce_sum x1, other arithmetic, on_device(): query_grad = jnp.sum(lax.all_gather(grad_term, ('dp', 'mp')), axis=0)  6.18 us
  transfers between devices with their start and end apart: 3, of which 2 were waited for; matrix products, arithmetic and copies ran while one was open for 9% of the time, Pallas kernels for 0%

profile of v1, /device:TPU:0, one launch (start us, length us, event | category | flops | bytes accessed | tf_op | source)
XLA Modules:
  0.0 280.5 jit_solution(9328596093787081352)
XLA Ops:
  7.2 2.0 copy.83
  15.9 5.7 %convolution_convert_fusion = bf16[64,1536]{1,0:T(8,128)(2,1)} fusion(bf16[1536,2048]{1,0:T(8,128)(2,1)} %param.19, bf16[1,128,2048]{2,1,0:T(8,128)(2,1)} %param.23, s32[]{:T(128)S(6)} %select_n.443), kind=kOutput, calls=%fused_computation.23 | convolution fusion | flops 402751488 | bytes 6750212 | tf_op jit(solution)/shard_map/ld,ed->le/dot_general | solution.py:156
  25.5 2.1 fusion.67
  29.2 2.1 broadcast_select_fusion.7
  33.5 1.4 convolution_select_fusion
  39.8 16.0 %all-reduce.2 = (f32[8]{0:T(128)}, f32[8]{0:T(128)S(1)}) all-reduce(f32[8]{0:T(128)S(1)} %dynamic-update-slice.2, f32[8]{0:T(128)S(1)} %dynamic-update-slice.3), channel_id=1, replica_groups=mesh['dp'=8,'mp'=4] {'dp'}, use_global_device_ids=true, to_apply=%add | all-reduce | flops 16 | bytes 128
  58.3 3.0 %fusion.20 = (f32[4,4,64]{2,1,0:T(4,128)S(1)}, f32[4,4,64]{2,1,0:T(4,128)S(1)}) fusion(f32[4,512,64,4]{1,2,3,0:T(8,128)} %copy-done.1, f32[4,4,64]{2,1,0:T(4,128)S(1)} %get-tuple-element.493, pred[512]{0:T(512)(128)(4,1)S(1)} %get-tuple-element.506, f32[4,4,64]{2,1,0:T(4,128)S(1)} %get-tuple-element.494, pred[512]{0:T(512)(128)(4,1)S(1)} %get-tuple-element.498), kind=kLoop, calls=%fused_computation.43 | loop fusion | flops 3143680 | bytes 2114560 | tf_op jit(solution)/shard_map/reduce_sum | solution.py:75
  61.3 8.3 %all-gather.1 = f32[32,4,64]{2,1,0:T(4,128)S(1)} all-gather(f32[4,4,64]{2,1,0:T(4,128)S(1)} %bitcast.201), channel_id=3, replica_groups=mesh['dp'=8,'mp'=4] {'dp'}, dimensions={0}, use_global_device_ids=true | all-gather | bytes 36864 | tf_op jit(solution)/shard_map/all_gather | solution.py:17
  69.6 9.4 %all-gather = f32[32,4,64]{2,1,0:T(4,128)S(1)} all-gather(f32[4,4,64]{2,1,0:T(4,128)S(1)} %copy-done.16), channel_id=2, replica_groups=mesh['dp'=8,'mp'=4] {'dp'}, dimensions={0}, use_global_device_ids=true | all-gather | bytes 36864 | tf_op jit(solution)/shard_map/all_gather | solution.py:17
  79.0 1.5 rev.19
  80.5 8.4 %all-gather.13.cloned.1.call-done = f32[32,4,64,96]{3,2,1,0:T(8,128)} async-done(((f32[4,4,64,96]{3,2,1,0:T(8,128)}), f32[32,4,64,96]{3,2,1,0:T(8,128)}) %all-gather.13.cloned.1.call-update) | async-done | bytes 3145744 | tf_op jit(solution)/shard_map/all_gather | solution.py:17
  88.9 34.2 %while.40 = (s32[]{:T(128)}, f32[]{:T(128)}, f32[4,4,64]{2,1,0:T(4,128)S(1)}, f32[4,4,64]{2,1,0:T(4,128)S(1)}, f32[4,4,64,96]{3,2,1,0:T(8,128)S(1)}, /*index=5*/...) while((s32[]{:T(128)}, f32[]{:T(128)}, ...), condition=%wide.region_10.11_spmd.clone, body=%wide.region_9.10_spmd.clone.sunk | while | flops 702472 | bytes 1220823 | solution.py:29
  91.5 1.6 select_select_fusion.14
  93.8 1.3 dynamic_slice.113
  96.4 1.6 select_select_fusion.14
  101.3 1.6 select_select_fusion.14
  106.2 1.6 select_select_fusion.14
  111.0 1.6 select_select_fusion.14
  115.9 1.6 select_select_fusion.14
  120.8 1.6 select_select_fusion.14
  123.9 9.1 %all-gather.4 = f32[32,4,64]{2,1,0:T(4,128)S(1)} all-gather(f32[4,4,64]{2,1,0:T(4,128)S(1)} %bitcast.191), channel_id=6, replica_groups=mesh['dp'=8,'mp'=4] {'dp'}, dimensions={0}, use_global_device_ids=true | all-gather | bytes 36864 | tf_op jit(solution)/shard_map/all_gather | solution.py:17
  133.0 2.4 fusion.42
  135.4 8.4 %all-gather.5 = f32[32,4,64]{2,1,0:T(4,128)S(1)} all-gather(f32[4,4,64]{2,1,0:T(4,128)S(1)} %get-tuple-element.502), channel_id=7, replica_groups=mesh['dp'=8,'mp'=4] {'dp'}, dimensions={0}, use_global_device_ids=true | all-gather | bytes 36864 | tf_op jit(solution)/shard_map/all_gather | solution.py:17
  143.7 9.3 %all-gather.3 = f32[32,4,64]{2,1,0:T(4,128)S(1)} all-gather(f32[4,4,64]{2,1,0:T(4,128)S(1)} %bitcast.197), channel_id=5, replica_groups=mesh['dp'=8,'mp'=4] {'dp'}, dimensions={0}, use_global_device_ids=true | all-gather | bytes 36864 | tf_op jit(solution)/shard_map/all_gather | solution.py:17
  153.1 9.4 %while.41 = (s32[]{:T(128)}, f32[4,4,64]{2,1,0:T(4,128)S(1)}, f32[4,4,64]{2,1,0:T(4,128)S(1)}, f32[4,4,64]{2,1,0:T(4,128)S(1)}, bf16[64,1536]{1,0:T(8,128)(2,1)S...) while((s32[]{:T(128)}, f32[4,4,64]{2,1,0:T(4,128)S(1)}, ...), condition=%wide.region_13.14_spmd.clone, body=%wide.region_12.13_spmd.clone.sunk | while | flops 304133 | bytes 626881 | solution.py:29
  164.5 1.4 fusion.47
  165.9 3.9 %fusion.25 = f32[64,4,4,96]{3,0,2,1:T(8,128)} fusion(bf16[512,4,96,1]{0,2,3,1:T(8,128)(2,1)} %bitcast.208, f32[4,4,64,512]{3,2,1,0:T(8,128)S(1)} %fusion.47, f32[4,512,64,4]{1,2,3,0:T(8,128)} %copy-done.1, bf16[512,4,96,1]{0,2,3,1:T(8,128)(2,1)S(1)} %bitcast.180, f32[4,4,64]{2,1,0:T(4,128)S(1)} %get-tuple-element.368, f32[4,4,64]{2,1,0:T(4,128)S(1)} %bitcast.203, ...), kind=kOutput, calls=%fused_computation.52 | convolution fusion | flops 206143488 | bytes 5595648 | tf_op jit(solution)/shard_map/gclr,rge->lgce/dot_general | solution.py:195
  169.7 1.5 copy.28
  172.9 4.0 %fusion.8 = bf16[1,64,2048]{2,1,0:T(8,128)(2,1)S(1)} fusion(bf16[64,1536]{1,0:T(8,128)(2,1)S(1)} %convert_element_type.70, bf16[1536,2048]{1,0:T(8,128)(2,1)} %param.19, bf16[1,128,2048]{2,1,0:T(8,128)(2,1)S(1)} %copy-done.6, s32[]{:T(128)S(6)} %select_n.443, pred[]{:T(512)S(6)} %le.3), kind=kOutput, calls=%fused_computation.26 | convolution fusion | flops 402915328 | bytes 7012357 | tf_op jit(solution)/shard_map/dot_general | solution.py:149
  176.9 1.4 select_n.447
  178.3 89.5 %all-gather.11.cloned.1.call-done = f32[32,64,1536]{2,1,0:T(8,128)} async-done(((f32[1,64,1536]{2,1,0:T(8,128)}), f32[32,64,1536]{2,1,0:T(8,128)}) %all-gather.11.cloned.1.call-update) | async-done | bytes 12582928 | tf_op jit(solution)/shard_map/all_gather | solution.py:199
  267.8 6.2 %reduce_sum.59 = f32[64,1536]{1,0:T(8,128)} reduce(f32[32,64,1536]{2,1,0:T(8,128)} %all-gather.11.cloned.1.call-done, f32[]{:T(128)} %constant.92.clone.1), dimensions={0}, to_apply=%region_14.15 | reduce | flops 3047424 | bytes 12976132 | tf_op jit(solution)/shard_map/reduce_sum | solution.py:199
  (136 shorter events, 30.1 us)
Async XLA Ops:
  7.2 20.4 %copy-start = (bf16[1152,384]{1,0:T(8,128)(2,1)S(1)}, bf16[1152,384]{1,0:T(8,128)(2,1)}, u32[]{:S(2)}) copy-start(bf16[1152,384]{1,0:T(8,128)(2,1)} %param.17) | copy-start | bytes 2654212
  7.2 71.9 %all-gather.15.cloned.1.call-start = ((), (), s32[]{:S(2)}) async-start(), calls=%async_computation.2 | async-start | bytes 1769472 | tf_op jit(solution)/shard_map/all_gather | solution.py:17
  15.8 8.4 %copy-start.12 = (bf16[64,1536]{1,0:T(8,128)(2,1)S(1)}, bf16[64,1536]{1,0:T(8,128)(2,1)}, u32[]{:S(2)}) copy-start(bf16[64,1536]{1,0:T(8,128)(2,1)} %param.16) | copy-start | bytes 589828
  15.8 9.4 %copy-start.8 = (bf16[1,512,1152]{2,1,0:T(8,128)(2,1)S(1)}, bf16[1,512,1152]{2,1,0:T(8,128)(2,1)}, u32[]{:S(2)}) copy-start(bf16[1,512,1152]{2,1,0:T(8,128)(2,1)} %param.14) | copy-start | bytes 3538948
  15.8 11.8 %copy-start.20 = (f32[1152]{0:T(1024)S(1)}, f32[1152]{0:T(1024)}, u32[]{:S(2)}) copy-start(f32[1152]{0:T(1024)} %param.15) | copy-start | bytes 13828
  21.6 67.4 %all-gather.13.cloned.1.call-start = ((), (), s32[]{:S(2)}) async-start(), calls=%async_computation.1 | async-start | bytes 4718592 | tf_op jit(solution)/shard_map/all_gather | solution.py:17
  25.5 3.0 %copy-start.11 = (bf16[64,4,4,96]{3,2,1,0:T(4,128)(2,1)S(1)}, bf16[64,4,4,96]{3,2,1,0:T(4,128)(2,1)}, u32[]{:S(2)}) copy-start(bf16[64,4,4,96]{3,2,1,0:T(4,128)(2,1)} %reshape.130) | copy-start | bytes 589828
  27.6 30.7 %copy-start.17 = (pred[512]{0:T(512)(128)(4,1)}, pred[512]{0:T(512)(128)(4,1)S(1)}, u32[]{:S(2)}) copy-start(pred[512]{0:T(512)(128)(4,1)S(1)} %get-tuple-element.498) | copy-start | bytes 1540
  28.4 3.6 %copy-start.21 = (bf16[512,384]{0,1:T(8,128)(2,1)}, bf16[512,384]{0,1:T(8,128)(2,1)S(1)}, u32[]{:S(2)}) copy-start(bf16[512,384]{0,1:T(8,128)(2,1)S(1)} %convolution_convert_fusion.3) | copy-start | bytes 1179652
  28.5 2.8 copy-start.9
  28.5 2.8 copy-start.19
  29.1 3.5 %copy-start.1 = (f32[4,512,64,4]{1,2,3,0:T(8,128)}, f32[4,512,64,4]{1,2,3,0:T(8,128)S(1)}, u32[]{:S(2)}) copy-start(f32[4,512,64,4]{1,2,3,0:T(8,128)S(1)} %get-tuple-element.509) | copy-start | bytes 6291460
  31.2 27.1 %copy-start.13 = (f32[4,4,64]{2,1,0:T(4,128)}, f32[4,4,64]{2,1,0:T(4,128)S(1)}, u32[]{:S(2)}) copy-start(f32[4,4,64]{2,1,0:T(4,128)S(1)} %get-tuple-element.494) | copy-start | bytes 12292
  32.1 0.7 copy-start.4
  32.7 0.9 copy-start.3
  32.7 4.9 %copy-start.23 = (u32[32]{0:T(128)S(1)}, u32[32]{0:T(128)}, u32[]{:S(2)}) copy-start(u32[32]{0:T(128)} %constant.109) | copy-start | bytes 388
  32.7 23.8 %copy-start.2 = (bf16[64,1536]{1,0:T(8,128)(2,1)S(1)}, bf16[64,1536]{1,0:T(8,128)(2,1)}, u32[]{:S(2)}) copy-start(bf16[64,1536]{1,0:T(8,128)(2,1)} %convolution_convert_fusion) | copy-start | bytes 589828
  34.9 34.6 %copy-start.16 = (f32[4,4,64]{2,1,0:T(4,128)S(1)}, f32[4,4,64]{2,1,0:T(4,128)}, u32[]{:S(2)}) copy-start(f32[4,4,64]{2,1,0:T(4,128)} %get-tuple-element.492) | copy-start | bytes 12292
  35.0 232.8 %all-gather.11.cloned.1.call-start = ((), (), s32[]{:S(2)}) async-start(), calls=%async_computation | async-start | bytes 12976128 | tf_op jit(solution)/shard_map/all_gather | solution.py:199
  123.8 29.2 %copy-start.14 = (f32[2,8,64]{2,1,0:T(8,128)}, f32[2,8,64]{2,1,0:T(8,128)S(1)}, u32[]{:S(2)}) copy-start(f32[2,8,64]{2,1,0:T(8,128)S(1)} %get-tuple-element.536) | copy-start | bytes 12292
  123.8 29.2 %copy-start.22 = (f32[8]{0:T(128)S(1)}, f32[8]{0:T(128)}, u32[]{:S(2)}) copy-start(f32[8]{0:T(128)} %rev.15) | copy-start | bytes 100
  153.1 11.4 %copy-start.5 = (bf16[512,384]{0,1:T(8,128)(2,1)S(1)}, bf16[512,384]{0,1:T(8,128)(2,1)}, u32[]{:S(2)}) copy-start(bf16[512,384]{0,1:T(8,128)(2,1)} %copy-done.4) | copy-start | bytes 1179652
  162.5 3.3 %copy-start.15 = (f32[2,8,64]{2,1,0:T(8,128)S(1)}, f32[2,8,64]{2,1,0:T(8,128)}, u32[]{:S(2)}) copy-start(f32[2,8,64]{2,1,0:T(8,128)} %copy-done.14) | copy-start | bytes 12292
  162.5 3.3 %copy-start.18 = (pred[512]{0:T(512)(128)(4,1)S(1)}, pred[512]{0:T(512)(128)(4,1)}, u32[]{:S(2)}) copy-start(pred[512]{0:T(512)(128)(4,1)} %copy-done.17) | copy-start | bytes 1540
  169.7 2.7 copy-start.10
  169.7 3.2 %copy-start.6 = (bf16[1,128,2048]{2,1,0:T(8,128)(2,1)S(1)}, bf16[1,128,2048]{2,1,0:T(8,128)(2,1)}, u32[]{:S(2)}) copy-start(bf16[1,128,2048]{2,1,0:T(8,128)(2,1)} %copy.83) | copy-start | bytes 1572868
  178.3 95.7 %copy-start.7 = (bf16[1,128,2048]{2,1,0:T(8,128)(2,1)}, bf16[1,128,2048]{2,1,0:T(8,128)(2,1)S(1)}, u32[]{:S(2)}) copy-start(bf16[1,128,2048]{2,1,0:T(8,128)(2,1)S(1)} %select_n.447) | copy-start | bytes 1572868
Sparse Core Ops, SparseCore 0:
  21.7 28.3 all-gather.14
  52.0 36.9 all-gather.12
  172.5 95.2 all-gather.10
